TPU v7x, 32 devices: a whole 2x2x4 slice. The times are simulated.
32 devices in a mesh: item: 8 (over z, y), code: 4 (over x, core).
Axes of the slice: x: 2, y: 2, z: 4, core: 2. Of those that a mesh axis runs over, the one named last changes fastest.
Arguments:
- residuals: float32 [256, 32768], P('code', 'item'), may hold values from -6 to 6
- codebook: float32 [256, 32768], P('item', 'code'), may hold values from -6 to 6
- item_weight: float32 [32768], P('item'), may hold values from 1 to 100
- code_capacity: float32 [32768], P('code'), may hold values from 0.25 to 4
- pairs: int32 [512, 64], P('item', 'code'), may hold values from -1 to 127, as said below
Outputs:
- item_potential: float32 [32768], P('item')
- code_potential: float32 [32768], P('code')
Inputs may be any that keep to these rules, and one draw needn't show every extreme that they name: `pairs`: each entry is -1 (no candidate) or a code block's number within the code shard of its slot column. Within one item block and one code shard the live entries are distinct, the first slot is always live, and between 1 and 8 are live; some device holds exactly 8 live slots in every item block. Every code block is named by some item block.
All inputs are finite; a program needn't handle non-finite values.
Results may differ from a plain program's by a relative error of at most 0.0003.
Values sent between devices are 32-bit elements; how exact they have to be, the bound alone decides.
No kernel may reach another device: no remote copies, remote signals or barrier semaphores. Data moves between devices by JAX's collectives and lax.ppermute only.
A program may use at most 128 MiB of HBM per device.

v0:
```python
import math
import jax
import jax.numpy as jnp
from jax import lax
from jax.sharding import PartitionSpec as P

BLOCK = 64
ITERS = 3
masked_score = -1e30
softness_factor = 0.1


def body(residuals, codebook, item_weight, code_capacity, pairs):
    item_columns = lax.all_gather(residuals, "code", axis=0, tiled=True)
    code_cols = lax.all_gather(codebook, "item", axis=0, tiled=True)
    embedding_width = item_columns.shape[0]
    item_count = item_columns.shape[1]
    code_count = code_cols.shape[1]
    item_blocks = item_count // BLOCK
    code_blocks = code_count // BLOCK
    logit_scale = 1.0 / (softness_factor * math.sqrt(embedding_width))
    weight_sum = lax.psum(jnp.sum(item_weight), "item")
    capacity_sum = lax.psum(jnp.sum(code_capacity), "code")
    item_logmass = jnp.log(item_weight) - jnp.log(weight_sum)
    code_logmass = jnp.log(code_capacity) - jnp.log(capacity_sum)
    slot_order = jnp.argsort((pairs < 0).astype(jnp.int32), axis=1, stable=True)[
        :, : pairs.shape[1] // 2
    ]
    chosen = jnp.take_along_axis(pairs, slot_order, axis=1)
    is_live = chosen >= 0
    safe_ids = jnp.where(is_live, chosen, 0)
    target = jnp.where(is_live, chosen, code_blocks)
    item_split_cols = item_columns.reshape(embedding_width, item_blocks, BLOCK)
    code_column_splits = code_cols.reshape(embedding_width, code_blocks, BLOCK)
    group = math.gcd(item_blocks, 8)
    group_count = item_blocks // group

    def build_tiles(own, ids, live):
        picked = code_column_splits[:, ids, :]
        scores = (
            jnp.einsum("rbi,rbsj->bsij", own, picked, precision=lax.Precision.HIGHEST) * logit_scale
        )
        return jnp.where(live[:, :, None, None], scores, masked_score)

    reduce_fn = lambda tiles, ids, portion: tiles

    def one_group(group_index):
        start = group_index * group
        own = lax.dynamic_slice_in_dim(item_split_cols, start, group, 1)
        ids = lax.dynamic_slice_in_dim(safe_ids, start, group, 0)
        live = lax.dynamic_slice_in_dim(is_live, start, group, 0)
        portion = lax.dynamic_slice_in_dim(safe_ids, start, group, 0)
        return reduce_fn(build_tiles(own, ids, live), ids, portion)

    results = lax.map(one_group, jnp.arange(group_count, dtype=jnp.int32))
    saved_tile_blocks = results.reshape((item_blocks,) + results.shape[2:])

    def run_pass(reduce_fn, extra):
        return reduce_fn(saved_tile_blocks, safe_ids, extra)

    flat_target = target.reshape(-1)
    flat_rows = flat_target.shape[0]
    row_group = math.gcd(flat_rows, 256)
    one_hot = flat_target[:, None] == jnp.arange(code_blocks, dtype=jnp.int32)[None, :]
    one_hot_groups = one_hot.reshape(flat_rows // row_group, row_group, code_blocks)
    one_hot_float = one_hot.astype(jnp.float32)
    code_potential = jnp.zeros((code_count,), jnp.float32)
    item_potential = jnp.zeros((item_count,), jnp.float32)
    for sweep in range(ITERS):
        code_split = code_potential.reshape(code_blocks, BLOCK)

        def row_reduce(tiles, ids, portion):
            logits = tiles + code_split[ids][:, :, None, :]
            block_peak = jnp.max(logits, axis=(1, 3))
            block_total = jnp.sum(jnp.exp(logits - block_peak[:, None, :, None]), axis=(1, 3))
            return (block_peak, block_total)

        row_peak, row_total = run_pass(row_reduce, safe_ids)
        row_peak = row_peak.reshape(item_count)
        row_total = row_total.reshape(item_count)
        merged_peak = lax.pmax(row_peak, "code")
        merged_total = lax.psum(row_total * jnp.exp(row_peak - merged_peak), "code")
        item_potential = item_logmass - (merged_peak + jnp.log(merged_total))
        item_split = item_potential.reshape(item_blocks, BLOCK)

        def col_reduce(tiles, ids, portion):
            logits = tiles + portion[:, None, :, None]
            block_peak = jnp.max(logits, axis=2)
            block_total = jnp.sum(jnp.exp(logits - block_peak[:, :, None, :]), axis=2)
            return (block_peak, block_total)

        tile_peak, tile_total = run_pass(col_reduce, item_split)
        peak_flat = tile_peak.reshape(flat_rows, BLOCK)
        total_flat = tile_total.reshape(flat_rows, BLOCK)
        peak_groups = peak_flat.reshape(flat_rows // row_group, row_group, BLOCK)

        def peak_step(carry, pieces):
            hot, peaks = pieces
            candidate = jnp.max(jnp.where(hot[:, :, None], peaks[:, None, :], masked_score), axis=0)
            return (jnp.maximum(carry, candidate), None)

        col_peak, unused = lax.scan(
            peak_step,
            jnp.full((code_blocks, BLOCK), masked_score, jnp.float32),
            (one_hot_groups, peak_groups),
        )
        padded_peak = jnp.concatenate(
            [col_peak, jnp.full((1, BLOCK), masked_score, jnp.float32)], axis=0
        )
        spread = total_flat * jnp.exp(peak_flat - padded_peak[flat_target])
        col_total = jnp.dot(
            one_hot_float.T,
            spread,
            precision=lax.Precision.HIGHEST,
            preferred_element_type=jnp.float32,
        )
        col_peak = col_peak.reshape(code_count)
        col_total = col_total.reshape(code_count)
        joined_peak = lax.pmax(col_peak, "item")
        joined_total = lax.psum(col_total * jnp.exp(col_peak - joined_peak), "item")
        code_potential = code_logmass - (joined_peak + jnp.log(joined_total))
    return (item_potential, code_potential)


def solution(mesh):
    placed = (P("code", "item"), P("item", "code"), P("item"), P("code"), P("item", "code"))
    return jax.shard_map(
        body, mesh=mesh, in_specs=placed, out_specs=(P("item"), P("code")), check_vma=False
    )
```

profile of v0, /device:TPU:0, one launch (start us, length us, event | category | flops | bytes accessed | tf_op | source)
XLA Modules:
  0.0 706.6 jit_solution(5821192888771860012)
XLA Ops:
  10.0 23.8 %psum.56 = f32[]{:T(128)} all-reduce(f32[]{:T(128)} %reduce_sum.72), channel_id=1, replica_groups=mesh['item'=8,'code'=4] {'item'}, use_global_device_ids=true, to_apply=%region_1.0 | all-reduce | flops 1 | bytes 8 | tf_op jit(solution)/shard_map/psum | solution.py:22
  52.4 121.0 %all-gather.3.cloned.1.call-done = f32[256,8192]{1,0:T(8,128)} async-done(((f32[32,8192]{1,0:T(8,128)}), f32[256,8192]{1,0:T(8,128)}) %all-gather.3.cloned.1.call-update) | async-done | bytes 8388624 | tf_op jit(solution)/shard_map/all_gather | solution.py:15
  173.4 9.0 %copy.37 = f32[256,8192]{0,1:T(8,128)} copy(f32[256,8192]{1,0:T(8,128)} %all-gather.3.cloned.1.call-done) | data formatting | bytes 16777216 | tf_op jit(solution)/shard_map/all_gather | solution.py:15
  182.4 120.6 %while.43 = (s32[]{:T(128)}, f32[8,8,8,64,64]{3,4,2,1,0:T(8,128)}, s32[8]{0:T(128)S(1)}, pred[64,8]{0,1:T(8,128)(4,1)S(1)}, s32[64,8]{0,1:T(8,128)S(1)}, /*index...) while((s32[]{:T(128)}, f32[8,8,8,64,64]{3,4,2,1,0:T(8,128)}, ...), condition=%wide.region_4.0_spmd, body=%wide.region_3.0_spmd.sunk | while | flops 805831872 | bytes 15212019 | solution.py:55
  302.9 9.4 %add_reduce_fusion.5 = f32[8,8,64]{2,1,0:T(8,128)S(1)} fusion(f32[8,8,8,64,64]{3,4,2,1,0:T(8,128)} %get-tuple-element.107, f32[8,8,8,64]{3,2,1,0:T(8,128)S(1)} %bitcast.97), kind=kLoop, calls=%fused_computation.39 | loop fusion | flops 4190208 | bytes 8536064 | tf_op jit(solution)/shard_map/reduce_max | solution.py:74
  319.0 10.2 %pmax.42 = f32[4096]{0:T(1024)S(1)} all-reduce(f32[4096]{0:T(1024)S(1)} %reshape.247), channel_id=1, replica_groups=mesh['item'=8,'code'=4] {'code'}, use_global_device_ids=true, to_apply=%region_8.9 | all-reduce | flops 4096 | bytes 32768 | tf_op jit(solution)/shard_map/pmax | solution.py:81
  329.2 11.4 %all-reduce.3 = (f32[4096]{0:T(1024)S(1)}, f32[]{:T(128)}) all-reduce(f32[4096]{0:T(1024)S(1)} %exponential_multiply_fusion.5, f32[]{:T(128)} %reduce_sum.73), channel_id=1, replica_groups=mesh['item'=8,'code'=4] {'code'}, use_global_device_ids=true, to_apply=%region_10.11 | all-reduce | flops 4097 | bytes 32776 | tf_op jit(solution)/shard_map/psum | solution.py:82
  340.7 8.2 %add_reduce_fusion.4 = f32[8,8,8,64]{3,2,1,0:T(8,128)S(1)} fusion(f32[8,8,8,64,64]{3,4,2,1,0:T(8,128)} %get-tuple-element.107, f32[8,8,64]{2,1,0:T(8,128)S(1)} %add.166), kind=kLoop, calls=%fused_computation.38 | loop fusion | flops 4161536 | bytes 8536064 | tf_op jit(solution)/shard_map/reduce_max | solution.py:88
  348.9 11.1 %exponential_reduce_fusion.4 = f32[8,8,8,64]{3,2,1,0:T(8,128)S(1)} fusion(f32[8,8,8,64,64]{3,4,2,1,0:T(8,128)} %get-tuple-element.107, f32[8,8,8,64]{3,2,1,0:T(8,128)S(1)} %add_reduce_fusion.4, f32[8,8,64]{2,1,0:T(8,128)S(1)} %add.166), kind=kLoop, calls=%fused_computation.32 | loop fusion | flops 6258688 | bytes 8667136 | tf_op jit(solution)/shard_map/reduce_sum | solution.py:89
  368.5 35.2 %pmax.43 = f32[8192]{0:T(1024)S(1)} all-reduce(f32[8192]{0:T(1024)S(1)} %reshape.249), channel_id=1, replica_groups=mesh['item'=8,'code'=4] {'item'}, use_global_device_ids=true, to_apply=%region_15.16 | all-reduce | flops 8192 | bytes 65536 | tf_op jit(solution)/shard_map/pmax | solution.py:119
  403.7 33.0 %psum.59 = f32[8192]{0:T(1024)S(1)} all-reduce(f32[8192]{0:T(1024)S(1)} %exponential_multiply_fusion.2), channel_id=1, replica_groups=mesh['item'=8,'code'=4] {'item'}, use_global_device_ids=true, to_apply=%region_17.18 | all-reduce | flops 8192 | bytes 65536 | tf_op jit(solution)/shard_map/psum | solution.py:120
  446.2 7.6 %exponential_reduce_fusion.3 = f32[8,8,64]{2,1,0:T(8,128)S(1)} fusion(f32[8,8,8,64,64]{3,4,2,1,0:T(8,128)} %get-tuple-element.107, f32[8,8,64]{2,1,0:T(8,128)S(1)} %add_reduce_fusion.3, f32[8,8,8,64]{3,2,1,0:T(8,128)S(1)} %bitcast.102), kind=kLoop, calls=%fused_computation.31 | loop fusion | flops 6287360 | bytes 8552448 | tf_op jit(solution)/shard_map/reduce_sum | solution.py:75
  454.0 10.1 %pmax.44 = f32[4096]{0:T(1024)S(1)} all-reduce(f32[4096]{0:T(1024)S(1)} %reshape.254), channel_id=1, replica_groups=mesh['item'=8,'code'=4] {'code'}, use_global_device_ids=true, to_apply=%region_19.20 | all-reduce | flops 4096 | bytes 32768 | tf_op jit(solution)/shard_map/pmax | solution.py:81
  464.1 10.1 %psum.60 = f32[4096]{0:T(1024)S(1)} all-reduce(f32[4096]{0:T(1024)S(1)} %exponential_multiply_fusion.4), channel_id=1, replica_groups=mesh['item'=8,'code'=4] {'code'}, use_global_device_ids=true, to_apply=%region_21.22 | all-reduce | flops 4096 | bytes 32768 | tf_op jit(solution)/shard_map/psum | solution.py:82
  474.3 8.2 %add_reduce_fusion.2 = f32[8,8,8,64]{3,2,1,0:T(8,128)S(1)} fusion(f32[8,8,8,64,64]{3,4,2,1,0:T(8,128)} %get-tuple-element.107, f32[8,8,64]{2,1,0:T(8,128)S(1)} %add.175), kind=kLoop, calls=%fused_computation.36 | loop fusion | flops 4161536 | bytes 8536064 | tf_op jit(solution)/shard_map/reduce_max | solution.py:88
  482.5 11.1 %exponential_reduce_fusion.2 = f32[8,8,8,64]{3,2,1,0:T(8,128)S(1)} fusion(f32[8,8,8,64,64]{3,4,2,1,0:T(8,128)} %get-tuple-element.107, f32[8,8,8,64]{3,2,1,0:T(8,128)S(1)} %add_reduce_fusion.2, f32[8,8,64]{2,1,0:T(8,128)S(1)} %add.175), kind=kLoop, calls=%fused_computation.30 | loop fusion | flops 6258688 | bytes 8667136 | tf_op jit(solution)/shard_map/reduce_sum | solution.py:89
  502.1 33.0 %pmax.45 = f32[8192]{0:T(1024)S(1)} all-reduce(f32[8192]{0:T(1024)S(1)} %reshape.256), channel_id=1, replica_groups=mesh['item'=8,'code'=4] {'item'}, use_global_device_ids=true, to_apply=%region_26.27 | all-reduce | flops 8192 | bytes 65536 | tf_op jit(solution)/shard_map/pmax | solution.py:119
  535.2 33.2 %psum.61 = f32[8192]{0:T(1024)S(1)} all-reduce(f32[8192]{0:T(1024)S(1)} %exponential_multiply_fusion.1), channel_id=1, replica_groups=mesh['item'=8,'code'=4] {'item'}, use_global_device_ids=true, to_apply=%region_28.29 | all-reduce | flops 8192 | bytes 65536 | tf_op jit(solution)/shard_map/psum | solution.py:120
  584.9 10.1 %pmax.46 = f32[4096]{0:T(1024)S(1)} all-reduce(f32[4096]{0:T(1024)S(1)} %reshape.261), channel_id=1, replica_groups=mesh['item'=8,'code'=4] {'code'}, use_global_device_ids=true, to_apply=%region_30.31 | all-reduce | flops 4096 | bytes 32768 | tf_op jit(solution)/shard_map/pmax | solution.py:81
  595.0 10.1 %psum.62 = f32[4096]{0:T(1024)S(1)} all-reduce(f32[4096]{0:T(1024)S(1)} %exponential_multiply_fusion.3), channel_id=1, replica_groups=mesh['item'=8,'code'=4] {'code'}, use_global_device_ids=true, to_apply=%region_32.33 | all-reduce | flops 4096 | bytes 32768 | tf_op jit(solution)/shard_map/psum | solution.py:82
  605.2 8.2 %add_reduce_fusion = f32[8,8,8,64]{3,2,1,0:T(8,128)S(1)} fusion(f32[8,8,8,64,64]{3,4,2,1,0:T(8,128)} %get-tuple-element.107, f32[8,8,64]{2,1,0:T(8,128)S(1)} %add.183), kind=kLoop, calls=%fused_computation.34 | loop fusion | flops 4161536 | bytes 8536064 | tf_op jit(solution)/shard_map/reduce_max | solution.py:88
  613.5 11.1 %exponential_reduce_fusion = f32[8,8,8,64]{3,2,1,0:T(8,128)S(1)} fusion(f32[8,8,8,64,64]{3,4,2,1,0:T(8,128)} %get-tuple-element.107, f32[8,8,8,64]{3,2,1,0:T(8,128)S(1)} %add_reduce_fusion, f32[8,8,64]{2,1,0:T(8,128)S(1)} %add.183), kind=kLoop, calls=%fused_computation.28 | loop fusion | flops 6258688 | bytes 8667136 | tf_op jit(solution)/shard_map/reduce_sum | solution.py:89
  633.1 33.0 %pmax.47 = f32[8192]{0:T(1024)S(1)} all-reduce(f32[8192]{0:T(1024)S(1)} %reshape.263), channel_id=1, replica_groups=mesh['item'=8,'code'=4] {'item'}, use_global_device_ids=true, to_apply=%region_37.38 | all-reduce | flops 8192 | bytes 65536 | tf_op jit(solution)/shard_map/pmax | solution.py:119
  666.1 33.0 %psum.63 = f32[8192]{0:T(1024)S(1)} all-reduce(f32[8192]{0:T(1024)S(1)} %exponential_multiply_fusion), channel_id=1, replica_groups=mesh['item'=8,'code'=4] {'item'}, use_global_device_ids=true, to_apply=%region_39.40 | all-reduce | flops 8192 | bytes 65536 | tf_op jit(solution)/shard_map/psum | solution.py:120
  (206 shorter events, 214.2 us)
Async XLA Ops:
  7.2 28.2 %copy-start = (s32[64,16]{0,1:T(8,128)S(1)}, s32[64,16]{0,1:T(8,128)}, u32[]{:S(2)}) copy-start(s32[64,16]{0,1:T(8,128)} %param.17) | copy-start | bytes 12292
  7.2 39.6 %all-gather.5.cloned.1.call-start = ((), (), s32[]{:S(2)}) async-start(), calls=%async_computation.1 | async-start | bytes 5242880 | tf_op jit(solution)/shard_map/all_gather | solution.py:14
  7.9 165.5 %all-gather.3.cloned.1.call-start = ((), (), s32[]{:S(2)}) async-start(), calls=%async_computation | async-start | bytes 9437184 | tf_op jit(solution)/shard_map/all_gather | solution.py:15
  35.4 4.6 copy-start.2
  302.9 10.7 %copy-start.1 = (f32[8,8,8,64,64]{3,4,2,1,0:T(8,128)S(1)}, f32[8,8,8,64,64]{3,4,2,1,0:T(8,128)}, u32[]{:S(2)}) copy-start(f32[8,8,8,64,64]{3,4,2,1,0:T(8,128)} %get-tuple-element.107) | copy-start | bytes 25165828
  302.9 37.6 %copy-start.3 = (f32[4096]{0:T(1024)S(1)}, f32[4096]{0:T(1024)}, u32[]{:S(2)}) copy-start(f32[4096]{0:T(1024)} %param.15) | copy-start | bytes 49156
  605.2 19.4 %copy-start.4 = (f32[4096]{0:T(1024)}, f32[4096]{0:T(1024)S(1)}, u32[]{:S(2)}) copy-start(f32[4096]{0:T(1024)S(1)} %add_subtract_fusion.3) | copy-start | bytes 49156
Sparse Core Ops, SparseCore 0:
  9.5 37.1 all-gather.4
  48.9 124.4 all-gather.2
where the time goes:
time: 708 us; the launch traced here: 707 us
  blocking collectives  286 us (40%)
  waiting for transfers between devices  127 us (18%)
  other arithmetic  127 us (18%)
  local copies, waits for them, and re-layouts  85.9 us (12%)
  matrix products  59.6 us (8%)
  between operations  15.8 us (2%)
    all_gather x1, waiting for transfers between devices, body(): code_cols = lax.all_gather(codebook, 'item', axis=0, tiled=True)  121 us
    pmax x3, blocking collectives, body(): joined_peak = lax.pmax(col_peak, 'item')  101 us
    psum x3, blocking collectives, body(): joined_total = lax.psum(col_total * jnp.exp(col_peak - joined_peak), 'item')  99.3 us
    dot_general x8, matrix products, build_tiles(): jnp.einsum('rbi,rbsj->bsij', own, picked, precision=lax.Precision.HIGHEST)  58.1 us
    gather x8, local copies, waits for them, and re-layouts, build_tiles(): picked = code_column_splits[:, ids, :]  49.4 us
    reduce_sum x3, other arithmetic, col_reduce(): block_total = jnp.sum(jnp.exp(logits - block_peak[:, :, None, :]), axis=2)  33.2 us
    psum x3, blocking collectives, body(): merged_total = lax.psum(row_total * jnp.exp(row_peak - merged_peak), 'code')  31.6 us
    pmax x3, blocking collectives, body(): merged_peak = lax.pmax(row_peak, 'code')  30.4 us
  transfers between devices with their start and end apart: 2, of which 2 were waited for; matrix products, arithmetic and copies ran while one was open for 2% of the time, Pallas kernels for 0%

commit v1 on v0

--- a/solution.py
+++ b/solution.py
@@ -12,7 +12,20 @@
 
 def body(residuals, codebook, item_weight, code_capacity, pairs):
     item_columns = lax.all_gather(residuals, "code", axis=0, tiled=True)
-    code_cols = lax.all_gather(codebook, "item", axis=0, tiled=True)
+
+    def draft_the_widths(original):
+        workers = lax.axis_size("item")
+        current_arr = [(i - 1, i) for i in range(1, workers)] + [(workers - 1, 0)]
+        z_new = original
+        heap = [z_new]
+        for _ in tuple(range(workers - 1)):
+            z_new = lax.ppermute(z_new, "item", current_arr)
+            heap += [z_new]
+        clean = jnp.concatenate([*reversed(heap)], 0)
+        vec_out = jnp.roll(clean, (lax.axis_index("item") + 1) * z_new.shape[0], 0)
+        return vec_out
+
+    code_cols = draft_the_widths(codebook)
     embedding_width = item_columns.shape[0]
     item_count = item_columns.shape[1]
     code_count = code_cols.shape[1]

time: 708 us -> 814 us (1.15)
  local copies, waits for them, and re-layouts: 85.9 us -> 160 us
  waiting for transfers between devices: 127 us -> 147 us
  blocking collectives: 286 us -> 295 us
    ppermute x0 -> x7, waiting for transfers between devices: none -> 147 us  [draft_the_widths(): z_new = lax.ppermute(z_new, 'item', current_arr)]
    all_gather x1 -> x0, waiting for transfers between devices: 121 us -> none  [body(): code_cols = lax.all_gather(codebook, 'item', axis=0, tiled=True)]
    concatenate x0 -> x1, local copies, waits for them, and re-layouts: none -> 46.3 us  [draft_the_widths(): vec_out = jnp.roll(clean, (lax.axis_index('item') + 1) * z_new.shape[0], 0)]
    ppermute x0 -> x7, local copies, waits for them, and re-layouts: none -> 23.3 us  [draft_the_widths(): z_new = lax.ppermute(z_new, 'item', current_arr)]
    dynamic_slice x0 -> x1, local copies, waits for them, and re-layouts: none -> 10 us  [draft_the_widths(): vec_out = jnp.roll(clean, (lax.axis_index('item') + 1) * z_new.shape[0], 0)]
    psum x1, blocking collectives: 23.8 us -> 33 us  [body(): weight_sum = lax.psum(jnp.sum(item_weight), 'item')]
    all_gather x1 -> x0, local copies, waits for them, and re-layouts: 9 us -> none  [body(): code_cols = lax.all_gather(codebook, 'item', axis=0, tiled=True)]
  transfers between devices with their start and end apart: 2 -> 8, of which waited for: 2 -> 6; matrix products, arithmetic and copies ran while one was open for 2% -> 5% of each run, Pallas kernels for 0% -> 0%
where the time goes in v1:
time: 814 us; the launch traced here: 811 us
  blocking collectives  295 us (36%)
  local copies, waits for them, and re-layouts  160 us (20%)
  waiting for transfers between devices  147 us (18%)
  other arithmetic  126 us (15%)
  matrix products  59.6 us (7%)
  between operations  15.9 us (2%)
    ppermute x7, waiting for transfers between devices, draft_the_widths(): z_new = lax.ppermute(z_new, 'item', current_arr)  147 us
    pmax x3, blocking collectives, body(): joined_peak = lax.pmax(col_peak, 'item')  101 us
    psum x3, blocking collectives, body(): joined_total = lax.psum(col_total * jnp.exp(col_peak - joined_peak), 'item')  99.3 us
    dot_general x8, matrix products, build_tiles(): jnp.einsum('rbi,rbsj->bsij', own, picked, precision=lax.Precision.HIGHEST)  58.1 us
    gather x8, local copies, waits for them, and re-layouts, build_tiles(): picked = code_column_splits[:, ids, :]  49 us
    concatenate x1, local copies, waits for them, and re-layouts, draft_the_widths(): vec_out = jnp.roll(clean, (lax.axis_index('item') + 1) * z_new.shape[0], 0)  46.3 us
    reduce_sum x3, other arithmetic, col_reduce(): block_total = jnp.sum(jnp.exp(logits - block_peak[:, :, None, :]), axis=2)  33.2 us
    psum x1, blocking collectives, body(): weight_sum = lax.psum(jnp.sum(item_weight), 'item')  33 us
  transfers between devices with their start and end apart: 8, of which 6 were waited for; matrix products, arithmetic and copies ran while one was open for 5% of the time, Pallas kernels for 0%

profile of v1, /device:TPU:0, one launch (start us, length us, event | category | flops | bytes accessed | tf_op | source)
XLA Modules:
  0.0 811.5 jit_solution(7034454668111535694)
XLA Ops:
  10.3 26.4 %collective-permute-done = f32[32,8192]{1,0:T(8,128)S(1)} collective-permute-done((f32[32,8192]{1,0:T(8,128)}, f32[32,8192]{1,0:T(8,128)S(1)}, u32[]{:S(2)}, u32[]{:S(2)}) %collective-permute-start) | collective-permute-done | bytes 1048608 | tf_op jit(solution)/shard_map/ppermute | solution.py:22
  36.7 27.0 %collective-permute-done.1 = f32[32,8192]{1,0:T(8,128)S(1)} collective-permute-done((f32[32,8192]{1,0:T(8,128)S(1)}, f32[32,8192]{1,0:T(8,128)S(1)}, u32[]{:S(2)}, u32[]{:S(2)}) %collective-permute-start.1) | collective-permute-done | bytes 1048608 | tf_op jit(solution)/shard_map/ppermute | solution.py:22
  63.7 26.2 %collective-permute-done.2 = f32[32,8192]{1,0:T(8,128)S(1)} collective-permute-done((f32[32,8192]{1,0:T(8,128)S(1)}, f32[32,8192]{1,0:T(8,128)S(1)}, u32[]{:S(2)}, u32[]{:S(2)}) %collective-permute-start.2) | collective-permute-done | bytes 1048608 | tf_op jit(solution)/shard_map/ppermute | solution.py:22
  89.9 25.3 %collective-permute-done.3 = f32[32,8192]{1,0:T(8,128)S(1)} collective-permute-done((f32[32,8192]{1,0:T(8,128)S(1)}, f32[32,8192]{1,0:T(8,128)S(1)}, u32[]{:S(2)}, u32[]{:S(2)}) %collective-permute-start.3) | collective-permute-done | bytes 1048608 | tf_op jit(solution)/shard_map/ppermute | solution.py:22
  116.2 24.6 %collective-permute-done.4 = f32[32,8192]{1,0:T(8,128)} collective-permute-done((f32[32,8192]{1,0:T(8,128)S(1)}, f32[32,8192]{1,0:T(8,128)}, u32[]{:S(2)}, u32[]{:S(2)}) %collective-permute-start.4) | collective-permute-done | bytes 1048608 | tf_op jit(solution)/shard_map/ppermute | solution.py:22
  147.6 17.2 %collective-permute-done.5 = f32[32,8192]{1,0:T(8,128)} collective-permute-done((f32[32,8192]{1,0:T(8,128)}, f32[32,8192]{1,0:T(8,128)}, u32[]{:S(2)}, u32[]{:S(2)}) %collective-permute-start.5) | collective-permute-done | bytes 1048608 | tf_op jit(solution)/shard_map/ppermute | solution.py:22
  164.7 33.0 %psum.56 = f32[]{:T(128)} all-reduce(f32[]{:T(128)} %reduce_sum.72), channel_id=1, replica_groups=mesh['item'=8,'code'=4] {'item'}, use_global_device_ids=true, to_apply=%region_1.2 | all-reduce | flops 1 | bytes 8 | tf_op jit(solution)/shard_map/psum | solution.py:35
  232.0 46.3 %concatenate.15 = f32[512,8192]{0,1:T(8,128)} concatenate(f32[32,8192]{0,1:T(8,128)} %copy.54, f32[32,8192]{0,1:T(8,128)} %copy.55, f32[32,8192]{0,1:T(8,128)} %copy.56, f32[32,8192]{0,1:T(8,128)} %copy.57, f32[32,8192]{0,1:T(8,128)} %copy.58, f32[32,8192]{0,1:T(8,128)} %copy.59, f32[32,8192]{0,1:T(8,128)} %copy.60, f32[32,8192]{0,1:T(8,128)} %copy.61, f32[32,8192]{0,1:T(8,128)} %copy.54, ...), dimensions={0} | concatenate | bytes 33554432 | tf_op jit(solution)/shard_map/jit(_roll_dynamic)/concatenate | solution.py:25
  288.3 119.5 %while.43 = (s32[]{:T(128)}, f32[8,8,8,64,64]{3,4,2,1,0:T(8,128)}, s32[8]{0:T(128)S(1)}, pred[64,8]{0,1:T(8,128)(4,1)S(1)}, s32[64,8]{0,1:T(8,128)S(1)}, /*index...) while((s32[]{:T(128)}, f32[8,8,8,64,64]{3,4,2,1,0:T(8,128)}, ...), condition=%wide.region_4.5_spmd, body=%wide.region_3.4_spmd.sunk | while | flops 805831872 | bytes 15212019 | solution.py:68
  423.9 10.2 %pmax.42 = f32[4096]{0:T(1024)S(1)} all-reduce(f32[4096]{0:T(1024)S(1)} %reshape.247), channel_id=1, replica_groups=mesh['item'=8,'code'=4] {'code'}, use_global_device_ids=true, to_apply=%region_8.9 | all-reduce | flops 4096 | bytes 32768 | tf_op jit(solution)/shard_map/pmax | solution.py:94
  434.1 11.4 %all-reduce.3 = (f32[4096]{0:T(1024)S(1)}, f32[]{:T(128)}) all-reduce(f32[4096]{0:T(1024)S(1)} %exponential_multiply_fusion.5, f32[]{:T(128)} %reduce_sum.73), channel_id=1, replica_groups=mesh['item'=8,'code'=4] {'code'}, use_global_device_ids=true, to_apply=%region_10.11 | all-reduce | flops 4097 | bytes 32776 | tf_op jit(solution)/shard_map/psum | solution.py:95
  453.8 11.1 %exponential_reduce_fusion.4 = f32[8,8,8,64]{3,2,1,0:T(8,128)S(1)} fusion(f32[8,8,8,64,64]{3,4,2,1,0:T(8,128)} %get-tuple-element.107, f32[8,8,8,64]{3,2,1,0:T(8,128)S(1)} %add_reduce_fusion.4, f32[8,8,64]{2,1,0:T(8,128)S(1)} %add.182), kind=kLoop, calls=%fused_computation.32 | loop fusion | flops 6258688 | bytes 8667136 | tf_op jit(solution)/shard_map/reduce_sum | solution.py:102
  473.4 35.1 %pmax.43 = f32[8192]{0:T(1024)S(1)} all-reduce(f32[8192]{0:T(1024)S(1)} %reshape.249), channel_id=1, replica_groups=mesh['item'=8,'code'=4] {'item'}, use_global_device_ids=true, to_apply=%region_15.16 | all-reduce | flops 8192 | bytes 65536 | tf_op jit(solution)/shard_map/pmax | solution.py:132
  508.6 33.0 %psum.59 = f32[8192]{0:T(1024)S(1)} all-reduce(f32[8192]{0:T(1024)S(1)} %exponential_multiply_fusion.2), channel_id=1, replica_groups=mesh['item'=8,'code'=4] {'item'}, use_global_device_ids=true, to_apply=%region_17.18 | all-reduce | flops 8192 | bytes 65536 | tf_op jit(solution)/shard_map/psum | solution.py:133
  558.8 10.1 %pmax.44 = f32[4096]{0:T(1024)S(1)} all-reduce(f32[4096]{0:T(1024)S(1)} %reshape.254), channel_id=1, replica_groups=mesh['item'=8,'code'=4] {'code'}, use_global_device_ids=true, to_apply=%region_19.20 | all-reduce | flops 4096 | bytes 32768 | tf_op jit(solution)/shard_map/pmax | solution.py:94
  568.9 10.1 %psum.60 = f32[4096]{0:T(1024)S(1)} all-reduce(f32[4096]{0:T(1024)S(1)} %exponential_multiply_fusion.4), channel_id=1, replica_groups=mesh['item'=8,'code'=4] {'code'}, use_global_device_ids=true, to_apply=%region_21.22 | all-reduce | flops 4096 | bytes 32768 | tf_op jit(solution)/shard_map/psum | solution.py:95
  587.4 11.1 %exponential_reduce_fusion.2 = f32[8,8,8,64]{3,2,1,0:T(8,128)S(1)} fusion(f32[8,8,8,64,64]{3,4,2,1,0:T(8,128)} %get-tuple-element.107, f32[8,8,8,64]{3,2,1,0:T(8,128)S(1)} %add_reduce_fusion.2, f32[8,8,64]{2,1,0:T(8,128)S(1)} %add.191), kind=kLoop, calls=%fused_computation.30 | loop fusion | flops 6258688 | bytes 8667136 | tf_op jit(solution)/shard_map/reduce_sum | solution.py:102
  607.0 33.0 %pmax.45 = f32[8192]{0:T(1024)S(1)} all-reduce(f32[8192]{0:T(1024)S(1)} %reshape.256), channel_id=1, replica_groups=mesh['item'=8,'code'=4] {'item'}, use_global_device_ids=true, to_apply=%region_26.27 | all-reduce | flops 8192 | bytes 65536 | tf_op jit(solution)/shard_map/pmax | solution.py:132
  640.0 33.2 %psum.61 = f32[8192]{0:T(1024)S(1)} all-reduce(f32[8192]{0:T(1024)S(1)} %exponential_multiply_fusion.1), channel_id=1, replica_groups=mesh['item'=8,'code'=4] {'item'}, use_global_device_ids=true, to_apply=%region_28.29 | all-reduce | flops 8192 | bytes 65536 | tf_op jit(solution)/shard_map/psum | solution.py:133
  689.8 10.1 %pmax.46 = f32[4096]{0:T(1024)S(1)} all-reduce(f32[4096]{0:T(1024)S(1)} %reshape.261), channel_id=1, replica_groups=mesh['item'=8,'code'=4] {'code'}, use_global_device_ids=true, to_apply=%region_30.31 | all-reduce | flops 4096 | bytes 32768 | tf_op jit(solution)/shard_map/pmax | solution.py:94
  699.9 10.1 %psum.62 = f32[4096]{0:T(1024)S(1)} all-reduce(f32[4096]{0:T(1024)S(1)} %exponential_multiply_fusion.3), channel_id=1, replica_groups=mesh['item'=8,'code'=4] {'code'}, use_global_device_ids=true, to_apply=%region_32.33 | all-reduce | flops 4096 | bytes 32768 | tf_op jit(solution)/shard_map/psum | solution.py:95
  718.3 11.1 %exponential_reduce_fusion = f32[8,8,8,64]{3,2,1,0:T(8,128)S(1)} fusion(f32[8,8,8,64,64]{3,4,2,1,0:T(8,128)} %get-tuple-element.107, f32[8,8,8,64]{3,2,1,0:T(8,128)S(1)} %add_reduce_fusion, f32[8,8,64]{2,1,0:T(8,128)S(1)} %add.199), kind=kLoop, calls=%fused_computation.28 | loop fusion | flops 6258688 | bytes 8667136 | tf_op jit(solution)/shard_map/reduce_sum | solution.py:102
  737.9 33.0 %pmax.47 = f32[8192]{0:T(1024)S(1)} all-reduce(f32[8192]{0:T(1024)S(1)} %reshape.263), channel_id=1, replica_groups=mesh['item'=8,'code'=4] {'item'}, use_global_device_ids=true, to_apply=%region_37.38 | all-reduce | flops 8192 | bytes 65536 | tf_op jit(solution)/shard_map/pmax | solution.py:132
  771.0 33.0 %psum.63 = f32[8192]{0:T(1024)S(1)} all-reduce(f32[8192]{0:T(1024)S(1)} %exponential_multiply_fusion), channel_id=1, replica_groups=mesh['item'=8,'code'=4] {'item'}, use_global_device_ids=true, to_apply=%region_39.40 | all-reduce | flops 8192 | bytes 65536 | tf_op jit(solution)/shard_map/psum | solution.py:133
  (236 shorter events, 289.2 us)
Async XLA Ops:
  7.2 135.2 %copy-start = (s32[64,16]{0,1:T(8,128)S(1)}, s32[64,16]{0,1:T(8,128)}, u32[]{:S(2)}) copy-start(s32[64,16]{0,1:T(8,128)} %param.17) | copy-start | bytes 12292
  7.2 215.7 %all-gather.2.cloned.1.call-start = ((), (), s32[]{:S(2)}) async-start(), calls=%async_computation | async-start | bytes 5242880 | tf_op jit(solution)/shard_map/all_gather | solution.py:14
  7.2 29.5 %collective-permute-start = (f32[32,8192]{1,0:T(8,128)}, f32[32,8192]{1,0:T(8,128)S(1)}, u32[]{:S(2)}, u32[]{:S(2)}) collective-permute-start(f32[32,8192]{1,0:T(8,128)} %param.14), channel_id=1, source_target_pairs={{0,4},{4,8},{8,12},{12,16},{16,20},{20,24},{24,28},{28,0},{1,5},{5... | collective-permute-start | bytes 3145736 | tf_op jit(solution)/shard_map/ppermute | solution.py:22
  36.7 27.0 %collective-permute-start.1 = (f32[32,8192]{1,0:T(8,128)S(1)}, f32[32,8192]{1,0:T(8,128)S(1)}, u32[]{:S(2)}, u32[]{:S(2)}) collective-permute-start(f32[32,8192]{1,0:T(8,128)S(1)} %collective-permute-done), channel_id=1, source_target_pairs={{0,4},{4,8},{8,12},{12,16},{16,20},{20,24},{24,28},{28,0},{1,5},{5... | collective-permute-start | bytes 3145736 | tf_op jit(solution)/shard_map/ppermute | solution.py:22
  63.7 26.2 %collective-permute-start.2 = (f32[32,8192]{1,0:T(8,128)S(1)}, f32[32,8192]{1,0:T(8,128)S(1)}, u32[]{:S(2)}, u32[]{:S(2)}) collective-permute-start(f32[32,8192]{1,0:T(8,128)S(1)} %collective-permute-done.1), channel_id=1, source_target_pairs={{0,4},{4,8},{8,12},{12,16},{16,20},{20,24},{24,28},{28,0},{1,5},{5... | collective-permute-start | bytes 3145736 | tf_op jit(solution)/shard_map/ppermute | solution.py:22
  89.9 52.3 %copy-start.3 = (f32[32,8192]{1,0:T(8,128)}, f32[32,8192]{1,0:T(8,128)S(1)}, u32[]{:S(2)}) copy-start(f32[32,8192]{1,0:T(8,128)S(1)} %collective-permute-done.2) | copy-start | bytes 3145732
  89.9 25.3 %collective-permute-start.3 = (f32[32,8192]{1,0:T(8,128)S(1)}, f32[32,8192]{1,0:T(8,128)S(1)}, u32[]{:S(2)}, u32[]{:S(2)}) collective-permute-start(f32[32,8192]{1,0:T(8,128)S(1)} %collective-permute-done.2), channel_id=1, source_target_pairs={{0,4},{4,8},{8,12},{12,16},{16,20},{20,24},{24,28},{28,0},{1,5},{5... | collective-permute-start | bytes 3145736 | tf_op jit(solution)/shard_map/ppermute | solution.py:22
  115.2 1.0 copy-start.4
  116.2 24.6 %collective-permute-start.4 = (f32[32,8192]{1,0:T(8,128)S(1)}, f32[32,8192]{1,0:T(8,128)}, u32[]{:S(2)}, u32[]{:S(2)}) collective-permute-start(f32[32,8192]{1,0:T(8,128)S(1)} %collective-permute-done.3), channel_id=1, source_target_pairs={{0,4},{4,8},{8,12},{12,16},{16,20},{20,24},{24,28},{28,0},{1,5},{5... | collective-permute-start | bytes 3145736 | tf_op jit(solution)/shard_map/ppermute | solution.py:22
  140.8 24.0 %collective-permute-start.5 = (f32[32,8192]{1,0:T(8,128)}, f32[32,8192]{1,0:T(8,128)}, u32[]{:S(2)}, u32[]{:S(2)}) collective-permute-start(f32[32,8192]{1,0:T(8,128)} %collective-permute-done.4), channel_id=1, source_target_pairs={{0,4},{4,8},{8,12},{12,16},{16,20},{20,24},{24,28},{28,0},{1,5},{5... | collective-permute-start | bytes 3145736 | tf_op jit(solution)/shard_map/ppermute | solution.py:22
  142.4 4.6 copy-start.7
  142.4 55.3 %copy-start.2 = (f32[32,8192]{1,0:T(8,128)S(1)}, f32[32,8192]{1,0:T(8,128)}, u32[]{:S(2)}) copy-start(f32[32,8192]{1,0:T(8,128)} %param.14) | copy-start | bytes 3145732
  142.4 58.2 %copy-start.5 = (f32[8192]{0:T(1024)S(1)}, f32[8192]{0:T(1024)}, u32[]{:S(2)}) copy-start(f32[8192]{0:T(1024)} %param.16) | copy-start | bytes 98308
  164.7 63.7 %collective-permute-start.6 = (f32[32,8192]{1,0:T(8,128)}, f32[32,8192]{1,0:T(8,128)}, u32[]{:S(2)}, u32[]{:S(2)}) collective-permute-start(f32[32,8192]{1,0:T(8,128)} %collective-permute-done.5), channel_id=1, source_target_pairs={{0,4},{4,8},{8,12},{12,16},{16,20},{20,24},{24,28},{28,0},{1,5},{5... | collective-permute-start | bytes 3145736 | tf_op jit(solution)/shard_map/ppermute | solution.py:22
  407.9 10.7 %copy-start.1 = (f32[8,8,8,64,64]{3,4,2,1,0:T(8,128)S(1)}, f32[8,8,8,64,64]{3,4,2,1,0:T(8,128)}, u32[]{:S(2)}) copy-start(f32[8,8,8,64,64]{3,4,2,1,0:T(8,128)} %get-tuple-element.107) | copy-start | bytes 25165828
  407.9 37.6 %copy-start.8 = (f32[4096]{0:T(1024)S(1)}, f32[4096]{0:T(1024)}, u32[]{:S(2)}) copy-start(f32[4096]{0:T(1024)} %param.15) | copy-start | bytes 49156
  453.8 88.5 %copy-start.6 = (f32[8192]{0:T(1024)S(1)}, f32[8192]{0:T(1024)}, u32[]{:S(2)}) copy-start(f32[8192]{0:T(1024)} %param.16) | copy-start | bytes 98308
  710.0 19.4 %copy-start.9 = (f32[4096]{0:T(1024)}, f32[4096]{0:T(1024)S(1)}, u32[]{:S(2)}) copy-start(f32[4096]{0:T(1024)S(1)} %add_subtract_fusion.3) | copy-start | bytes 49156
Sparse Core Ops, SparseCore 0:
  36.8 35.8 all-gather.1
